TPU v7x, 512 devices: a whole 4x4x16 slice. The times are simulated.
512 devices in a mesh: rows: 128 (over x, z, core), rep: 4 (over y).
Axes of the slice: x: 4, y: 4, z: 16, core: 2. Of those that a mesh axis runs over, the one named last changes fastest.
Arguments:
- feats: bfloat16 [4, 32768, 512], P('rep', 'rows'), may hold values from -24 to 24
- grad_out: bfloat16 [4, 32768, 512], P('rep', 'rows'), may hold values from -6 to 6
- qkv_weight: bfloat16 [512, 1536], P('rows'), may hold values from -0.25 to 0.25
- proj_weight: bfloat16 [512, 512], P('rows'), may hold values from -0.25 to 0.25
- to_hilbert: int32 [4, 16384], P('rep', 'rows'), may hold values from 0 to 16383, as said below
- to_zorder: int32 [4, 16384], P('rep', 'rows'), may hold values from 0 to 16383, as said below
Outputs:
- grad_feats: bfloat16 [4, 32768, 512], P('rep', 'rows')
- qkv_grad: float32 [512, 1536], P('rows')
- proj_grad: float32 [512, 512], P('rows')
Inputs may be any that keep to these rules, and one draw needn't show every extreme that they name: to_hilbert[s] is a permutation of the blocks of scene s and to_zorder[s] its inverse; of the 128 Z-order blocks of one device, at most 2 have Hilbert positions on any one device, and exactly 2 for some pair of devices in every scene. `to_zorder`: the inverse of to_hilbert in every scene.
All inputs are finite; a program needn't handle non-finite values.
Results may differ from a plain program's by a relative error of at most 0.015.
The roundings to bfloat16 on the way count: a program that leaves them out, or rounds other values in their place, can miss the bound.
Values may be sent and summed in bfloat16 or wider, within the bound.
No kernel may reach another device: no remote copies, remote signals or barrier semaphores. Data moves between devices by JAX's collectives and lax.ppermute only.
A program may use at most 64 MiB of HBM per device.

v0:
```python
import jax
import jax.numpy as jnp
from jax import lax
from jax.sharding import PartitionSpec as P

HEADS = 8
CAP = 2


def from_partner(block, axis, apart):
    count = lax.axis_size(axis)
    route = []
    for low in range(count):
        high = low | 1 << apart
        if high != low and high < count:
            route += [(low, high), (high, low)]
    return lax.ppermute(block, axis, route)


def move_blocks(outgoing):
    return lax.all_to_all(outgoing, "rows", split_axis=0, concat_axis=0, tiled=True)


def rank_within(order_keys, owners):
    same_owner = owners[None, :] == owners[:, None]
    earlier = order_keys[None, :] < order_keys[:, None]
    return jnp.sum(jnp.logical_and(same_owner, earlier).astype(jnp.int32), axis=1)


def contract_rows(left, right):
    return lax.dot_general(
        left, right, (((0,), (0,)), ((), ())), preferred_element_type=jnp.float32
    )


def contract_cols(left, right):
    return lax.dot_general(
        left, right, (((1,), (1,)), ((), ())), preferred_element_type=jnp.float32
    )


def per_device(feats, grad_out, qkv_weight, proj_weight, to_hilbert, to_zorder):
    peer_count = lax.axis_size("rows")
    feature = feats[0]
    rows_dev, channels = feature.shape
    head_size = channels // HEADS
    scale = head_size ** (-0.5)
    blocks_dev = to_hilbert.shape[1]
    slot_count = peer_count * CAP
    w_qkv, w_proj = (
        lax.all_gather(qkv_weight, "rows", axis=0, tiled=True),
        lax.all_gather(proj_weight, "rows", axis=0, tiled=True),
    )
    forward_list = to_hilbert[0]
    inverse_list = to_zorder[0]
    local_ids = jnp.arange(blocks_dev, dtype=jnp.int32)
    slot_ids = jnp.arange(slot_count, dtype=jnp.int32)
    target_dev = forward_list // blocks_dev
    send_slot = target_dev * CAP + rank_within(local_ids, target_dev)
    send_table = (send_slot[None, :] == slot_ids[:, None]).astype(jnp.bfloat16)
    source_dev = inverse_list // blocks_dev
    recv_slot = source_dev * CAP + rank_within(inverse_list, source_dev)
    recv_table = (recv_slot[:, None] == slot_ids[None, :]).astype(jnp.bfloat16)
    zblocks = grad_out[0].reshape(blocks_dev, -1)
    outgoing = jnp.dot(send_table, zblocks, preferred_element_type=jnp.float32).astype(jnp.bfloat16)
    arrived = move_blocks(outgoing.reshape(peer_count, CAP, -1)).reshape(slot_count, -1)
    grad_hil = jnp.dot(recv_table, arrived, preferred_element_type=jnp.float32).astype(jnp.bfloat16)
    grad_hil = grad_hil.reshape(rows_dev, channels)
    qkv = jnp.dot(feature, w_qkv, preferred_element_type=jnp.float32).astype(jnp.bfloat16)
    query = qkv[:, :channels]
    keyval = qkv[:, channels:]
    grad_attn = contract_cols(grad_hil, w_proj).astype(jnp.bfloat16)
    other_kv = from_partner(keyval, "rows", 0)
    keys_all = jnp.concatenate([keyval[:, :channels], other_kv[:, :channels]], axis=0)
    values_all = jnp.concatenate([keyval[:, channels:], other_kv[:, channels:]], axis=0)
    attn_parts, dq_parts, dk_parts, dv_parts = ([], [], [], [])
    for head_index in range(HEADS):
        lo_col = head_index * head_size
        q_head = query[:, lo_col : lo_col + head_size]
        k_head = keys_all[:, lo_col : lo_col + head_size]
        v_head = values_all[:, lo_col : lo_col + head_size]
        g_head = grad_attn[:, lo_col : lo_col + head_size]
        score = contract_cols(q_head, k_head) * scale
        row_max = jnp.max(score, axis=1, keepdims=True)
        raised = jnp.exp(score - row_max)
        row_sum = jnp.sum(raised, axis=1, keepdims=True)
        probs = raised / row_sum
        probs_b = probs.astype(jnp.bfloat16)
        attn_parts.append(
            jnp.dot(probs_b, v_head, preferred_element_type=jnp.float32).astype(jnp.bfloat16)
        )
        dprob = contract_cols(g_head, v_head)
        delta = jnp.sum(probs * dprob, axis=1, keepdims=True)
        dscore = (probs * (dprob - delta) * scale).astype(jnp.bfloat16)
        dq_parts.append(jnp.dot(dscore, k_head, preferred_element_type=jnp.float32))
        dk_parts.append(contract_rows(dscore, q_head))
        dv_parts.append(contract_rows(probs_b, g_head))
    grad_q = jnp.concatenate(dq_parts, axis=1)
    grad_k = jnp.concatenate(dk_parts, axis=1)
    grad_v = jnp.concatenate(dv_parts, axis=1)
    other_k, other_v = (
        from_partner(grad_k[rows_dev:].astype(jnp.bfloat16), "rows", 0).astype(jnp.float32),
        from_partner(grad_v[rows_dev:].astype(jnp.bfloat16), "rows", 0).astype(jnp.float32),
    )
    grad_k = grad_k[:rows_dev] + other_k
    grad_v = grad_v[:rows_dev] + other_v
    grad_qkv = jnp.concatenate([grad_q, grad_k, grad_v], axis=1).astype(jnp.bfloat16)
    attn = jnp.concatenate(attn_parts, axis=1)
    grad_hfeat = contract_cols(grad_qkv, w_qkv).astype(jnp.bfloat16)
    hblocks = grad_hfeat.reshape(blocks_dev, -1)
    going_back = contract_rows(recv_table, hblocks).astype(jnp.bfloat16)
    returned = move_blocks(going_back.reshape(peer_count, CAP, -1)).reshape(slot_count, -1)
    grad_z = contract_rows(send_table, returned).astype(jnp.bfloat16).reshape(rows_dev, channels)
    share = channels // peer_count
    term = jnp.concatenate(
        [contract_rows(feature, grad_qkv), contract_rows(attn, grad_hil)], axis=1
    )
    total = lax.psum(term, ("rows", "rep"))
    owned = lax.dynamic_slice_in_dim(total, lax.axis_index("rows") * share, share, 0)
    return (grad_z[None], owned[:, : 3 * channels], owned[:, 3 * channels :])


def solution(mesh):
    placed = (
        P("rep", "rows", None),
        P("rep", "rows", None),
        P("rows", None),
        P("rows", None),
        P("rep", "rows"),
        P("rep", "rows"),
    )
    return jax.shard_map(
        per_device,
        mesh=mesh,
        in_specs=placed,
        out_specs=(P("rep", "rows", None), P("rows", None), P("rows", None)),
        check_vma=False,
    )
```

profile of v0, /device:TPU:2, one launch (start us, length us, event | category | flops | bytes accessed | tf_op | source)
XLA Modules:
  0.0 721.0 jit_solution(14029525855574183305)
XLA Ops:
  7.2 0.7 all-gather.4.cloned.1.call-update
  7.9 1.0 reshape_squeeze.3
  9.0 0.7 and_select_fusion.2
  9.6 0.7 fusion.202
  10.5 0.7 fusion.113
  11.5 1.0 reshape.119
  12.5 19.5 %all-to-all-start = ((bf16[128,2,1024]{2,1,0:T(2,128)(2,1)}), bf16[128,2,1024]{2,1,0:T(2,128)(2,1)S(1)}, u32[]{:S(2)}, u32[]{:S(2)}) async-start(bf16[128,2,1024]{2,1,0:T(2,128)(2,1)} %reshape.119), calls=%async_computation | async-start | bytes 1048576 | tf_op jit(solution)/shard_map/all_to_all | solution.py:21
  32.0 100.5 %all-gather.1 = bf16[128,4,512]{2,1,0:T(4,128)(2,1)S(1)} all-gather(bf16[1,4,512]{2,1,0:T(4,128)(2,1)S(1)} %bitcast.64), channel_id=1, replica_groups=mesh['rows'=128,'rep'=4] {'rows'}, dimensions={0}, use_global_device_ids=true | all-gather | bytes 528384 | tf_op jit(solution)/shard_map/all_gather | solution.py:52
  132.9 1.0 reshape.120
  133.9 22.9 %all-gather.4.cloned.1.call-done = bf16[128,4,1536]{2,1,0:T(4,128)(2,1)} async-done(((bf16[1,4,1536]{2,1,0:T(4,128)(2,1)}), bf16[128,4,1536]{2,1,0:T(4,128)(2,1)}) %all-gather.4.cloned.1.call-update) | async-done | bytes 1572880 | tf_op jit(solution)/shard_map/all_gather | solution.py:51
  156.9 2.7 reshape.126
  159.6 0.6 convolution_convert_fusion
  160.2 0.9 slice.187
  161.0 2.3 collective-permute-start
  163.4 1.0 convolution_convert_fusion.6
  164.4 1.0 reshape.121
  165.4 0.3 convolution_convert_fusion.5
  165.8 1.1 fusion.160
  167.0 0.3 fusion.161
  167.6 0.3 fusion.7
  168.0 0.3 multiply_reduce_fusion.7
  168.6 0.4 fusion.162
  169.0 0.3 fusion.163
  169.3 0.4 fusion.164
  169.7 0.3 fusion.165
  170.0 0.4 fusion.166
  170.4 0.3 fusion.167
  171.4 0.4 fusion.168
  172.0 0.4 multiply_reduce_fusion.6
  172.4 0.3 convolution_dynamic-update-slice_fusion.6
  172.7 0.4 fusion.6
  173.3 0.3 multiply_reduce_fusion.5
  173.9 0.3 fusion.5
  174.5 0.4 multiply_reduce_fusion.4
  174.9 0.3 convolution_dynamic-update-slice_fusion.4
  175.2 0.4 fusion.4
  175.8 0.3 multiply_reduce_fusion.3
  176.9 0.4 multiply_reduce_fusion.2
  177.3 0.3 convolution_dynamic-update-slice_fusion.2
  177.7 0.4 fusion.2
  178.3 0.3 multiply_reduce_fusion.1
  179.1 0.4 multiply_reduce_fusion
  179.5 0.3 convolution_dynamic-update-slice_fusion
  179.8 0.3 fusion.1
  180.1 0.3 fusion
  180.5 2.1 collective-permute-start.2
  182.6 1.3 fusion.169
  188.6 2.4 collective-permute-start.1
  191.4 0.6 collective-permute-done.1
  192.2 1.3 convolution_convert_fusion.4
  193.6 0.6 convolution_bitcast_fusion
  194.1 1.7 reshape.122
  195.8 2.2 convolution_convert_fusion.1
  198.0 2.1 reshape.123
  200.1 12.8 %all-to-all-start.1 = ((bf16[128,2,1024]{2,1,0:T(2,128)(2,1)}), bf16[128,2,1024]{2,1,0:T(2,128)(2,1)}, u32[]{:S(2)}, u32[]{:S(2)}) async-start(bf16[128,2,1024]{2,1,0:T(2,128)(2,1)} %reshape.123), calls=%async_computation.1 | async-start | bytes 1048576 | tf_op jit(solution)/shard_map/all_to_all | solution.py:21
  212.9 3.6 pad_maximum_fusion
  216.5 29.6 %all-to-all-done.1 = bf16[128,2,1024]{2,1,0:T(2,128)(2,1)} async-done(((bf16[128,2,1024]{2,1,0:T(2,128)(2,1)}), bf16[128,2,1024]{2,1,0:T(2,128)(2,1)}, u32[]{:S(2)}, u32[]{:S(2)}) %all-to-all-start.1) | async-done | bytes 524320 | tf_op jit(solution)/shard_map/all_to_all | solution.py:21
  246.2 1.2 reshape.124
  247.7 0.8 broadcast_in_dim_reshape.3
  248.5 461.6 %all-reduce.2.cloned.1.call-done = f32[512,2048]{0,1:T(8,128)} async-done(((f32[512,2048]{0,1:T(8,128)}), f32[512,2048]{0,1:T(8,128)}) %all-reduce.2.cloned.1.call-update) | async-done | bytes 4194320 | tf_op jit(solution)/shard_map/psum | solution.py:118
  710.0 1.4 constant_dynamic-slice_fusion
  711.4 0.9 copy.13
  712.3 1.1 dynamic-slice.1
  713.4 0.7 copy.14
  (66 shorter events, 10.6 us)
Async XLA Ops:
  7.2 152.4 %copy-start = (bf16[1,256,512]{2,1,0:T(8,128)(2,1)S(1)}, bf16[1,256,512]{2,1,0:T(8,128)(2,1)}, u32[]{:S(2)}) copy-start(bf16[1,256,512]{2,1,0:T(8,128)(2,1)} %param.6) | copy-start | bytes 786436
  7.2 24.8 %copy-start.2 = (bf16[4,512]{1,0:T(4,128)(2,1)S(1)}, bf16[4,512]{1,0:T(4,128)(2,1)}, u32[]{:S(2)}) copy-start(bf16[4,512]{1,0:T(4,128)(2,1)} %param.9) | copy-start | bytes 12292
  7.2 125.5 %copy-start.3 = (s32[1,128]{1,0:T(1,128)S(1)}, s32[1,128]{1,0:T(1,128)}, u32[]{:S(2)}) copy-start(s32[1,128]{1,0:T(1,128)} %param.11) | copy-start | bytes 1540
  7.2 149.7 %all-gather.4.cloned.1.call-start = ((), (), s32[]{:S(2)}) async-start(), calls=%async_computation.3 | async-start | bytes 1585152 | tf_op jit(solution)/shard_map/all_gather | solution.py:51
  12.5 120.5 %all-to-all-start = ((bf16[128,2,1024]{2,1,0:T(2,128)(2,1)}), bf16[128,2,1024]{2,1,0:T(2,128)(2,1)S(1)}, u32[]{:S(2)}, u32[]{:S(2)}) async-start(bf16[128,2,1024]{2,1,0:T(2,128)(2,1)} %reshape.119), calls=%async_computation | async-start | bytes 1048576 | tf_op jit(solution)/shard_map/all_to_all | solution.py:21
  159.6 3.8 copy-start.1
  161.0 4.8 collective-permute-start
  180.5 11.7 %collective-permute-start.2 = (bf16[256,512]{0,1:T(8,128)(2,1)S(1)}, bf16[256,512]{0,1:T(8,128)(2,1)S(1)}, u32[]{:S(2)}, u32[]{:S(2)}) collective-permute-start(bf16[256,512]{0,1:T(8,128)(2,1)S(1)} %slice.454), channel_id=1, source_target_pairs={{0,4},{4,0},{8,12},{12,8},{16,20},{20,16},{24,28},{28,24},{32,36},... | collective-permute-start | bytes 786440 | tf_op jit(solution)/shard_map/ppermute | solution.py:17
  188.6 3.4 collective-permute-start.1
  200.1 46.1 %all-to-all-start.1 = ((bf16[128,2,1024]{2,1,0:T(2,128)(2,1)}), bf16[128,2,1024]{2,1,0:T(2,128)(2,1)}, u32[]{:S(2)}, u32[]{:S(2)}) async-start(bf16[128,2,1024]{2,1,0:T(2,128)(2,1)} %reshape.123), calls=%async_computation.1 | async-start | bytes 1048576 | tf_op jit(solution)/shard_map/all_to_all | solution.py:21
  212.9 497.2 %all-reduce.2.cloned.1.call-start = ((), (), s32[]{:S(2)}) async-start(), calls=%async_computation.2 | async-start | bytes 8388608 | tf_op jit(solution)/shard_map/psum | solution.py:118
Sparse Core Ops, SparseCore 0:
  11.1 145.7 all-gather.3
  219.2 490.8 all-reduce.1
where the time goes:
time: 722 us; the launch traced here: 721 us
  waiting for transfers between devices  515 us (71%)
  blocking collectives  101 us (14%)
  starting transfers between devices  39.3 us (5%)
  matrix products  22.5 us (3%)
  local copies, waits for them, and re-layouts  18.9 us (3%)
  between operations  14.4 us (2%)
  other arithmetic  9.94 us (1%)
    psum x1, waiting for transfers between devices, per_device(): total = lax.psum(term, ('rows', 'rep'))  462 us
    all_gather x1, blocking collectives, per_device(): lax.all_gather(proj_weight, 'rows', axis=0, tiled=True)  101 us
    all_to_all x2, starting transfers between devices, move_blocks(): lax.all_to_all(outgoing, 'rows', split_axis=0, concat_axis=0, tiled=True)  32.3 us
    all_to_all x2, waiting for transfers between devices, move_blocks(): lax.all_to_all(outgoing, 'rows', split_axis=0, concat_axis=0, tiled=True)  29.6 us
    all_gather x1, waiting for transfers between devices, per_device(): lax.all_gather(qkv_weight, 'rows', axis=0, tiled=True)  22.9 us
  transfers between devices with their start and end apart: 7, of which 4 were waited for; matrix products, arithmetic and copies ran while one was open for 3% of the time, Pallas kernels for 0%

commit v1 on v0

--- a/solution.py
+++ b/solution.py
@@ -40,6 +40,12 @@
 
 
 def per_device(feats, grad_out, qkv_weight, proj_weight, to_hilbert, to_zorder):
+
+    def play_object_here(unit, group_axis, d0):
+        block_out = jnp.stack([unit for _ in range(lax.axis_size(group_axis))], axis=0)
+        ready = lax.all_to_all(block_out, group_axis, 0, 0)
+        return jnp.concatenate(ready, d0)
+
     peer_count = lax.axis_size("rows")
     feature = feats[0]
     rows_dev, channels = feature.shape
@@ -48,7 +54,7 @@
     blocks_dev = to_hilbert.shape[1]
     slot_count = peer_count * CAP
     w_qkv, w_proj = (
-        lax.all_gather(qkv_weight, "rows", axis=0, tiled=True),
+        play_object_here(qkv_weight, group_axis="rows", d0=0),
         lax.all_gather(proj_weight, "rows", axis=0, tiled=True),
     )
     forward_list = to_hilbert[0]

time: 722 us -> 786 us (1.089)
  blocking collectives: 101 us -> 198 us
  waiting for transfers between devices: 515 us -> 492 us
  starting transfers between devices: 39.3 us -> 28.9 us
    all_to_all x0 -> x1, blocking collectives: none -> 53 us  [move_blocks(): lax.all_to_all(outgoing, 'rows', split_axis=0, concat_axis=0, tiled=True)]
    all_gather x1, blocking collectives: 101 us -> 145 us  [per_device(): lax.all_gather(proj_weight, 'rows', axis=0, tiled=True)]
    all_gather x1 -> x0, waiting for transfers between devices: 22.9 us -> none  [per_device(): lax.all_gather(qkv_weight, 'rows', axis=0, tiled=True)]
    all_to_all x2 -> x1, starting transfers between devices: 32.3 us -> 14.7 us  [move_blocks(): lax.all_to_all(outgoing, 'rows', split_axis=0, concat_axis=0, tiled=True)]
    all_to_all x2 -> x1, waiting for transfers between devices: 29.6 us -> 29.6 us  [move_blocks(): lax.all_to_all(outgoing, 'rows', split_axis=0, concat_axis=0, tiled=True)]
  transfers between devices with their start and end apart: 7 -> 6, of which waited for: 4 -> 3; matrix products, arithmetic and copies ran while one was open for 3% -> 2% of each run, Pallas kernels for 0% -> 0%
where the time goes in v1:
time: 786 us; the launch traced here: 785 us
  waiting for transfers between devices  492 us (63%)
  blocking collectives  198 us (25%)
  starting transfers between devices  28.9 us (4%)
  matrix products  22.5 us (3%)
  local copies, waits for them, and re-layouts  19.7 us (3%)
  between operations  14.4 us (2%)
  other arithmetic  9.98 us (1%)
    psum x1, waiting for transfers between devices, per_device(): total = lax.psum(term, ('rows', 'rep'))  462 us
    all_gather x1, blocking collectives, per_device(): lax.all_gather(proj_weight, 'rows', axis=0, tiled=True)  145 us
    all_to_all x1, blocking collectives, move_blocks(): lax.all_to_all(outgoing, 'rows', split_axis=0, concat_axis=0, tiled=True)  53 us
    all_to_all x1, waiting for transfers between devices, move_blocks(): lax.all_to_all(outgoing, 'rows', split_axis=0, concat_axis=0, tiled=True)  29.6 us
  transfers between devices with their start and end apart: 6, of which 3 were waited for; matrix products, arithmetic and copies ran while one was open for 2% of the time, Pallas kernels for 0%

profile of v1, /device:TPU:2, one launch (start us, length us, event | category | flops | bytes accessed | tf_op | source)
XLA Modules:
  0.0 784.9 jit_solution(11317120249204379902)
XLA Ops:
  7.2 0.7 and_select_fusion.2
  7.9 0.7 fusion.202
  8.7 0.7 fusion.113
  9.4 1.0 reshape_squeeze.3
  11.0 53.0 %all_to_all.15 = bf16[128,2,1024]{2,1,0:T(2,128)(2,1)S(1)} all-to-all(bf16[128,2,1024]{2,1,0:T(2,128)(2,1)S(1)} %reshape.125), channel_id=1, replica_groups=mesh['rows'=128,'rep'=4] {'rows'}, dimensions={0} | all-to-all | bytes 1048576 | tf_op jit(solution)/shard_map/all_to_all | solution.py:21
  63.9 1.6 stack.2
  65.5 7.3 all-to-all-start
  72.8 144.6 %all-gather = bf16[128,4,512]{2,1,0:T(4,128)(2,1)S(1)} all-gather(bf16[1,4,512]{2,1,0:T(4,128)(2,1)S(1)} %bitcast.62), channel_id=1, replica_groups=mesh['rows'=128,'rep'=4] {'rows'}, dimensions={0}, use_global_device_ids=true | all-gather | bytes 528384 | tf_op jit(solution)/shard_map/all_gather | solution.py:58
  217.7 1.0 reshape.126
  218.7 2.7 reshape.124
  221.4 0.6 convolution_convert_fusion
  222.0 0.9 slice.187
  222.9 2.4 collective-permute-start
  225.3 1.0 convolution_convert_fusion.6
  226.3 1.0 reshape.127
  227.3 0.3 convolution_convert_fusion.5
  227.7 1.1 fusion.160
  228.9 0.3 fusion.161
  229.6 0.3 fusion.7
  229.9 0.3 multiply_reduce_fusion.7
  230.5 0.4 fusion.162
  230.9 0.3 fusion.163
  231.2 0.4 fusion.164
  231.6 0.3 fusion.165
  231.9 0.4 fusion.166
  232.3 0.3 fusion.167
  233.3 0.4 fusion.168
  233.9 0.4 multiply_reduce_fusion.6
  234.3 0.3 convolution_dynamic-update-slice_fusion.6
  234.6 0.4 fusion.6
  235.2 0.3 multiply_reduce_fusion.5
  235.8 0.3 fusion.5
  236.4 0.4 multiply_reduce_fusion.4
  236.8 0.3 convolution_dynamic-update-slice_fusion.4
  237.1 0.4 fusion.4
  237.7 0.3 multiply_reduce_fusion.3
  238.3 0.3 fusion.3
  238.8 0.4 multiply_reduce_fusion.2
  239.2 0.3 convolution_dynamic-update-slice_fusion.2
  239.6 0.4 fusion.2
  240.2 0.3 multiply_reduce_fusion.1
  241.0 0.4 multiply_reduce_fusion
  241.4 0.3 convolution_dynamic-update-slice_fusion
  241.7 0.3 fusion.1
  242.0 0.3 fusion
  242.4 2.1 collective-permute-start.2
  244.4 1.3 fusion.169
  250.4 2.5 collective-permute-start.1
  253.3 0.5 collective-permute-done.1
  254.1 1.3 convolution_convert_fusion.4
  255.4 0.6 convolution_bitcast_fusion
  256.0 1.7 reshape.128
  257.7 2.2 convolution_convert_fusion.1
  259.8 2.1 reshape.129
  261.9 14.7 %all-to-all-start.2 = ((bf16[128,2,1024]{2,1,0:T(2,128)(2,1)}), bf16[128,2,1024]{2,1,0:T(2,128)(2,1)}, u32[]{:S(2)}, u32[]{:S(2)}) async-start(bf16[128,2,1024]{2,1,0:T(2,128)(2,1)} %reshape.129), calls=%async_computation.2 | async-start | bytes 1048576 | tf_op jit(solution)/shard_map/all_to_all | solution.py:21
  276.7 3.6 pad_maximum_fusion
  280.3 29.6 %all-to-all-done.2 = bf16[128,2,1024]{2,1,0:T(2,128)(2,1)} async-done(((bf16[128,2,1024]{2,1,0:T(2,128)(2,1)}), bf16[128,2,1024]{2,1,0:T(2,128)(2,1)}, u32[]{:S(2)}, u32[]{:S(2)}) %all-to-all-start.2) | async-done | bytes 524320 | tf_op jit(solution)/shard_map/all_to_all | solution.py:21
  309.9 1.2 reshape.130
  311.4 0.8 broadcast_in_dim_reshape.3
  312.2 461.7 %all-reduce.2.cloned.1.call-done = f32[512,2048]{0,1:T(8,128)} async-done(((f32[512,2048]{0,1:T(8,128)}), f32[512,2048]{0,1:T(8,128)}) %all-reduce.2.cloned.1.call-update) | async-done | bytes 4194320 | tf_op jit(solution)/shard_map/psum | solution.py:124
  773.9 1.4 constant_dynamic-slice_fusion
  775.3 0.9 copy.13
  776.2 1.1 dynamic-slice.1
  777.3 0.7 copy.14
  (67 shorter events, 10.5 us)
Async XLA Ops:
  7.2 214.3 %copy-start = (bf16[1,256,512]{2,1,0:T(8,128)(2,1)S(1)}, bf16[1,256,512]{2,1,0:T(8,128)(2,1)}, u32[]{:S(2)}) copy-start(bf16[1,256,512]{2,1,0:T(8,128)(2,1)} %param.6) | copy-start | bytes 786436
  10.4 53.5 %copy-start.2 = (bf16[4,1536]{1,0:T(4,128)(2,1)S(1)}, bf16[4,1536]{1,0:T(4,128)(2,1)}, u32[]{:S(2)}) copy-start(bf16[4,1536]{1,0:T(4,128)(2,1)} %param.8) | copy-start | bytes 36868
  65.5 7.3 copy-start.3
  65.5 153.2 %all-to-all-start = ((bf16[128,4,1536]{2,1,0:T(4,128)(2,1)}), bf16[128,4,1536]{2,1,0:T(4,128)(2,1)}, u32[]{:S(2)}, u32[]{:S(2)}) async-start(bf16[128,4,1536]{2,1,0:T(4,128)(2,1)} %stack.2), calls=%async_computation | async-start | bytes 3145728 | tf_op jit(solution)/shard_map/all_to_all | solution.py:46
  72.7 144.7 %copy-start.4 = (s32[1,128]{1,0:T(1,128)S(1)}, s32[1,128]{1,0:T(1,128)}, u32[]{:S(2)}) copy-start(s32[1,128]{1,0:T(1,128)} %param.11) | copy-start | bytes 1540
  221.4 3.9 copy-start.1
  222.9 4.8 collective-permute-start
  242.4 11.6 %collective-permute-start.2 = (bf16[256,512]{0,1:T(8,128)(2,1)S(1)}, bf16[256,512]{0,1:T(8,128)(2,1)S(1)}, u32[]{:S(2)}, u32[]{:S(2)}) collective-permute-start(bf16[256,512]{0,1:T(8,128)(2,1)S(1)} %slice.454), channel_id=1, source_target_pairs={{0,4},{4,0},{8,12},{12,8},{16,20},{20,16},{24,28},{28,24},{32,36},... | collective-permute-start | bytes 786440 | tf_op jit(solution)/shard_map/ppermute | solution.py:17
  250.4 3.4 collective-permute-start.1
  261.9 48.0 %all-to-all-start.2 = ((bf16[128,2,1024]{2,1,0:T(2,128)(2,1)}), bf16[128,2,1024]{2,1,0:T(2,128)(2,1)}, u32[]{:S(2)}, u32[]{:S(2)}) async-start(bf16[128,2,1024]{2,1,0:T(2,128)(2,1)} %reshape.129), calls=%async_computation.2 | async-start | bytes 1048576 | tf_op jit(solution)/shard_map/all_to_all | solution.py:21
  276.6 497.3 %all-reduce.2.cloned.1.call-start = ((), (), s32[]{:S(2)}) async-start(), calls=%async_computation.3 | async-start | bytes 8388608 | tf_op jit(solution)/shard_map/psum | solution.py:124
Sparse Core Ops, SparseCore 0:
  282.9 491.0 all-reduce.1
